TPU v7x, 32 devices: a whole 2x2x4 slice. The times are simulated.
32 devices in a mesh: group: 2 (over x), seq: 4 (over y, core), fsdp: 4 (over z).
Axes of the slice: x: 2, y: 2, z: 4, core: 2. Of those that a mesh axis runs over, the one named last changes fastest.
Arguments:
- latents: bfloat16 [8192, 3072], P(('group', 'seq', 'fsdp')), parts along dimension 0, may hold values from -6 to 6
- qkv_weight: bfloat16 [3072, 3, 3072], P('seq', None, 'fsdp'), may hold values from -0.109375 to 0.109375
- out_weight: bfloat16 [3072, 3072], P('fsdp', 'seq'), may hold values from -0.109375 to 0.109375
- mod_weight: bfloat16 [256, 3, 3072], P(None, None, ('seq', 'fsdp')), may hold values from -1 to 1
- q_gain: float32 [128], replicated, may hold values from 0.5 to 12, as said below
- k_gain: float32 [128], replicated, may hold values from 0.5 to 12, as said below
- tile_slot: int32 [8, 16], P('group'), parts along dimension 0, may hold values from 0 to 15, each once within a row
- win_start: int32 [8, 16, 3], P('group'), parts along dimension 0, may hold values from 0 to 2, as said below
- step_index: int32 [2], P('group'), parts along dimension 0, may hold values from 0 to 999
Outputs:
- updated: bfloat16 [8192, 3072], P(('group', 'seq', 'fsdp')), parts along dimension 0
There are 2 independent parts, one for each index of `group`. A program takes and returns all parts, laid end to end along the dimension named above; an argument that names none is the same for every part. Nothing has to cross between parts.
Inputs may be any that keep to these rules, and one draw needn't show every extreme that they name: win_start[t, p] holds the first time slice, tile row and tile column of the window of the tile at spatial position p (row p // 4, column p % 4) of slice t; the window spans 2 slices, 3 rows and 3 columns inside the clip and contains the tile itself. `tile_slot`: each row is an ordering of the 16 spatial tiles. `q_gain`: positive gains. `k_gain`: positive gains.
All inputs are finite; a program needn't handle non-finite values.
Results may differ from a plain program's by a relative error of at most 0.014.
The roundings to bfloat16 on the way count: a program that leaves them out, or rounds other values in their place, can miss the bound.
Values may be sent and summed in bfloat16 or wider, within the bound.
A program may use at most 192 MiB of HBM per device.

v0:
```python
import math
import jax
import jax.numpy as jnp
from jax import lax
from jax.sharding import PartitionSpec as P

HD = 128
FREQ = 256
TILE = 64
GW = 4


def with_halo(block, sides, width):
    for axis, dim in sides:
        count = lax.axis_size(axis)
        forward = [(i, i + 1) for i in range(count - 1)]
        backward = [(target, source) for source, target in forward]
        low = lax.ppermute(
            lax.slice_in_dim(block, block.shape[dim] - width, None, axis=dim), axis, forward
        )
        high = lax.ppermute(lax.slice_in_dim(block, 0, width, axis=dim), axis, backward)
        block = jnp.concatenate([low, block, high], axis=dim)
    return block


def time_signal(step_index):
    halfway = FREQ // 2
    freqs_all = jnp.exp(-math.log(10000.0) * jnp.arange(halfway, dtype=jnp.float32) / halfway)
    angles = step_index[0].astype(jnp.float32) * freqs_all
    return jax.nn.silu(jnp.concatenate([jnp.cos(angles), jnp.sin(angles)])).astype(jnp.bfloat16)


def modulate(tokens_in, shift_mod, scale_mod):
    values = tokens_in.astype(jnp.float32)
    centre = jnp.mean(values, axis=-1, keepdims=True)
    spread = jnp.mean((values - centre) ** 2, axis=-1, keepdims=True)
    normal = (values - centre) * lax.rsqrt(spread + 1e-06)
    return (normal * (1.0 + scale_mod) + shift_mod).astype(jnp.bfloat16)


def rms_scale(values, gain_vec):
    return values * lax.rsqrt(jnp.mean(values * values, axis=-1, keepdims=True) + 1e-06) * gain_vec


def project_rows(normed, weight_flat, q_gain, k_gain):
    mixture = jnp.dot(normed, weight_flat, preferred_element_type=jnp.float32)
    row_count = normed.shape[0]
    mixture = mixture.reshape(row_count, 3, -1, HD)
    queries = rms_scale(mixture[:, 0], q_gain)
    key_vecs = rms_scale(mixture[:, 1], k_gain)
    return (
        jnp.stack([queries, key_vecs, mixture[:, 2]], axis=1)
        .reshape(row_count, -1)
        .astype(jnp.bfloat16)
    )


def slot_masks(tile_slot, win_start, block_idx):
    blocks_total = tile_slot.shape[0]
    spot_count = tile_slot.shape[1]
    ids_query = lax.dynamic_index_in_dim(tile_slot, block_idx, 0, keepdims=False)
    window_row = lax.dynamic_index_in_dim(win_start, block_idx, 0, keepdims=False)
    onehot = ids_query[:, None] == jnp.arange(spot_count, dtype=jnp.int32)[None, :]
    corner = jnp.sum(jnp.where(onehot[:, :, None], window_row[None], 0), axis=1)
    result = []
    for offset in (-1, 0, 1):
        key_time = block_idx + offset
        ids_key = lax.dynamic_index_in_dim(
            tile_slot, jnp.clip(key_time, 0, blocks_total - 1), 0, keepdims=False
        )
        tile_row = ids_key // GW
        tile_col = ids_key % GW
        inside = (corner[:, 0:1] <= key_time) & (key_time <= corner[:, 0:1] + 1)
        inside = (
            inside & (corner[:, 1:2] <= tile_row[None]) & (tile_row[None] <= corner[:, 1:2] + 2)
        )
        inside = (
            inside & (corner[:, 2:3] <= tile_col[None]) & (tile_col[None] <= corner[:, 2:3] + 2)
        )
        result.append(jnp.repeat(jnp.repeat(inside, TILE, axis=0), TILE, axis=1))
    return result


def body(
    latents, qkv_weight, out_weight, mod_weight, q_gain, k_gain, tile_slot, win_start, step_index
):
    signal = time_signal(step_index)
    local_cols = mod_weight.shape[2]
    own_mod = jnp.dot(
        signal[None], mod_weight.reshape(FREQ, 3 * local_cols), preferred_element_type=jnp.float32
    ).reshape(3, local_cols)
    modulation = lax.all_gather(own_mod, ("seq", "fsdp"), axis=1, tiled=True)
    shift_mod = modulation[0]
    scale_mod = modulation[1]
    gate_mod = modulation[2]
    qkv_full = lax.all_gather(qkv_weight, "seq", axis=0, tiled=True)
    out_full = lax.all_gather(out_weight, "seq", axis=1, tiled=True)
    model_width = qkv_full.shape[0]
    group_width = qkv_full.shape[2]
    head_count = group_width // HD
    weight_flat = qkv_full.reshape(model_width, 3 * group_width)
    packed = project_rows(
        modulate(lax.all_gather(latents, "fsdp", axis=0, tiled=True), shift_mod, scale_mod),
        weight_flat,
        q_gain,
        k_gain,
    )
    block_tokens = packed.shape[0]
    query_all = packed[:, :group_width].reshape(block_tokens, head_count, HD)
    kv_local = packed[:, group_width:]
    extended = with_halo(kv_local[None], (("seq", 0),), 1)
    key_all = extended[:, :, :group_width].reshape(3, block_tokens, head_count, HD)
    value_all = extended[:, :, group_width:].reshape(3, block_tokens, head_count, HD)
    visible = slot_masks(tile_slot, win_start, lax.axis_index("seq"))
    inv_root = 1.0 / math.sqrt(HD)
    query_span = 512
    head_outputs = []
    for head_idx in range(head_count):
        row_parts = []
        for query_blk in range(block_tokens // query_span):
            lower = query_blk * query_span
            queries = query_all[lower : lower + query_span, head_idx]
            running_top = jnp.full((query_span,), -1e30, jnp.float32)
            running_total = jnp.zeros((query_span,), jnp.float32)
            accum = jnp.zeros((query_span, HD), jnp.float32)
            for key_blk in range(3):
                scores = (
                    lax.dot_general(
                        queries,
                        key_all[key_blk, :, head_idx],
                        (((1,), (1,)), ((), ())),
                        preferred_element_type=jnp.float32,
                    )
                    * inv_root
                )
                allowed = visible[key_blk][lower : lower + query_span]
                shifted = jnp.where(allowed, scores, -1e30)
                new_top = jnp.maximum(running_top, jnp.max(shifted, axis=1))
                weights = jnp.where(allowed, jnp.exp(shifted - new_top[:, None]), 0.0)
                factor = jnp.exp(running_top - new_top)
                running_total = running_total * factor + jnp.sum(weights, axis=1)
                accum = accum * factor[:, None] + jnp.dot(
                    weights.astype(jnp.bfloat16),
                    value_all[key_blk, :, head_idx],
                    preferred_element_type=jnp.float32,
                )
                running_top = new_top
            row_parts.append(accum / running_total[:, None])
        head_outputs.append(jnp.concatenate(row_parts, axis=0))
    attended = (
        jnp.stack(head_outputs, axis=1).reshape(block_tokens, group_width).astype(jnp.bfloat16)
    )
    projected = lax.psum_scatter(
        jnp.dot(attended, out_full, preferred_element_type=jnp.float32).astype(jnp.bfloat16),
        "fsdp",
        scatter_dimension=0,
        tiled=True,
    ).astype(jnp.float32)
    return (latents.astype(jnp.float32) + gate_mod * projected).astype(jnp.bfloat16)


def solution(mesh):
    in_specs = (
        P(("group", "seq", "fsdp"), None),
        P("seq", None, "fsdp"),
        P("fsdp", "seq"),
        P(None, None, ("seq", "fsdp")),
        P(),
        P(),
        P("group", None),
        P("group", None, None),
        P("group"),
    )
    out_specs = P(("group", "seq", "fsdp"), None)
    return jax.shard_map(body, mesh=mesh, in_specs=in_specs, out_specs=out_specs, check_vma=False)
```

profile of v0, /device:TPU:0, one launch (start us, length us, event | category | flops | bytes accessed | tf_op | source)
XLA Modules:
  0.0 624.4 jit_solution(11329790541286253678)
XLA Ops:
  7.3 6.1 copy.163
  14.4 37.1 %all-gather = f32[16,192,3]{1,2,0:T(4,128)S(1)} all-gather(f32[1,192,3]{1,2,0:T(4,128)S(1)} %bitcast.464), channel_id=1, replica_groups=mesh['group'=2,'seq'=4,'fsdp'=4] {'seq','fsdp'}, dimensions={0}, use_global_device_ids=true | all-gather | bytes 39168 | tf_op jit(solution)/shard_map/all_gather | solution.py:92
  52.3 75.7 %all-gather.5.cloned.1.call-done = bf16[1024,3072]{1,0:T(8,128)(2,1)} async-done(((bf16[256,3072]{1,0:T(8,128)(2,1)}), bf16[1024,3072]{1,0:T(8,128)(2,1)}) %all-gather.5.cloned.1.call-update) | async-done | bytes 6291472 | tf_op jit(solution)/shard_map/all_gather | solution.py:103
  127.9 3.8 convert_reduce_fusion
  134.3 84.6 %all-gather.7.cloned.1.call-done = bf16[3072,3,768]{0,2,1:T(8,128)(2,1)} async-done(((bf16[768,3,768]{0,2,1:T(8,128)(2,1)}), bf16[3072,3,768]{0,2,1:T(8,128)(2,1)}) %all-gather.7.cloned.1.call-update) | async-done | bytes 14155792 | tf_op jit(solution)/shard_map/all_gather | solution.py:96
  218.9 20.0 %fusion.7 = f32[1024,3,6,128]{0,3,2,1:T(8,128)S(1)} fusion(bf16[3,6,128,3072]{3,2,1,0:T(8,128)(2,1)} %bitcast.468, bf16[1024,3072]{1,0:T(8,128)(2,1)} %all-gather.5.cloned.1.call-done, f32[3072]{0:T(1024)S(1)} %bitcast.465, f32[3072]{0:T(1024)S(1)} %bitcast.466, f32[1024]{0:T(1024)S(1)} %add_rsqrt_fusion.2, f32[1024]{0:T(1024)S(1)} %broadcast_multiply_fusion), kind=kOutput, calls=%fused_computation.10 | convolution fusion | flops 14514388992 | bytes 29917184 | tf_op jit(solution)/shard_map/dot_general | solution.py:46
  244.4 3.9 collective-permute-start
  249.6 12.3 %reduce-scatter.2.cloned.1.call-start = ((), (), s32[]{:S(2)}) async-start(), calls=%async_computation.4 | async-start | bytes 7864320 | tf_op jit(solution)/shard_map/reduce_scatter | solution.py:153
  275.4 7.7 %pad_maximum_fusion = bf16[3,1024,1536]{1,2,0:T(8,128)(2,1)} fusion(bf16[1,1024,1536]{1,2,0:T(8,128)(2,1)} %collective-permute-done.1, bf16[1,1024,1536]{1,2,0:T(8,128)(2,1)S(1)} %slice_bitcast_fusion, bf16[1,1024,1536]{1,2,0:T(8,128)(2,1)} %collective-permute-done), kind=kLoop, calls=%fused_computation.8 | loop fusion | flops 9437184 | bytes 18874368 | tf_op jit(solution)/shard_map/concatenate | solution.py:22
  283.1 7.2 %fusion.406 = (bf16[3,1024,768]{1,2,0:T(8,128)(2,1)}, bf16[3,1024,768]{1,2,0:T(8,128)(2,1)S(1)}) fusion(bf16[3,1024,1536]{1,2,0:T(8,128)(2,1)} %pad_maximum_fusion), kind=kLoop, calls=%fused_computation.634 | loop fusion | bytes 18874368 | tf_op jit(solution)/shard_map/slice | solution.py:113
  325.7 5.0 fusion.43
  330.7 5.3 fusion.44
  336.1 4.7 fusion.45
  340.9 10.0 %fusion.109 = (f32[512]{0:T(512)S(1)}, f32[512]{0:T(512)S(1)}, f32[512]{0:T(512)S(1)}, f32[512]{0:T(512)S(1)}, f32[512]{0:T(512)S(1)}, /*index=5*/f32[512]{0:T(512)S(1)}) fusion(pred[512,1024]{1,0:T(32,128)(4,1)} %copy.164, f32[512,1024]{1,0:T(8,128)} %get-tuple-element.202, f32[512]{0:T(512)S(1)} %get-tuple-element.167, f32[512]{0:T(512)S(1)} %get-tuple-element.166, ...), kind=kLoop, calls=%fused_computation.192 | loop fusion | flops 15725568 | bytes 13131776 | tf_op jit(solution)/shard_map/reduce_sum | solution.py:141
  350.8 6.6 %fusion.111 = (f32[512]{0:T(512)S(1)}, f32[512]{0:T(512)S(1)}, f32[512]{0:T(512)S(1)}, f32[512]{0:T(512)S(1)}, f32[512]{0:T(512)S(1)}, /*index=5*/f32[512]{0:T(512)S(1)}) fusion(pred[512,1024]{1,0:T(32,128)(4,1)S(1)} %copy-done.28, f32[512,1024]{1,0:T(8,128)} %get-tuple-element.201, f32[512]{0:T(512)S(1)} %get-tuple-element.121, ...), kind=kLoop, calls=%fused_computation.194 | loop fusion | flops 15725568 | bytes 13131776 | tf_op jit(solution)/shard_map/reduce_sum | solution.py:141
  357.4 6.6 %fusion.113 = (f32[512]{0:T(512)S(1)}, f32[512]{0:T(512)S(1)}, f32[512]{0:T(512)S(1)}, f32[512]{0:T(512)S(1)}, f32[512]{0:T(512)S(1)}, /*index=5*/f32[512]{0:T(512)S(1)}) fusion(pred[512,1024]{1,0:T(32,128)(4,1)S(1)} %copy-done.29, f32[512,1024]{1,0:T(8,128)} %get-tuple-element.200, f32[512]{0:T(512)S(1)} %get-tuple-element.120, ...), kind=kLoop, calls=%fused_computation.196 | loop fusion | flops 15725568 | bytes 13131776 | tf_op jit(solution)/shard_map/reduce_sum | solution.py:141
  370.6 5.3 fusion.46
  376.0 4.7 fusion.47
  380.7 4.7 fusion.48
  385.4 10.2 %fusion.115 = (f32[512]{0:T(512)S(1)}, f32[512]{0:T(512)S(1)}, f32[512]{0:T(512)S(1)}, f32[512]{0:T(512)S(1)}, f32[512]{0:T(512)S(1)}, /*index=5*/f32[512]{0:T(512)S(1)}) fusion(pred[512,1024]{1,0:T(32,128)(4,1)} %copy.170, f32[512,1024]{1,0:T(8,128)} %get-tuple-element.199, f32[512]{0:T(512)S(1)} %get-tuple-element.180, f32[512]{0:T(512)S(1)} %get-tuple-element.179, ...), kind=kLoop, calls=%fused_computation.198 | loop fusion | flops 15725568 | bytes 13131776 | tf_op jit(solution)/shard_map/reduce_sum | solution.py:141
  395.7 9.3 %fusion.117 = (f32[512]{0:T(512)S(1)}, f32[512]{0:T(512)S(1)}, f32[512]{0:T(512)S(1)}, f32[512]{0:T(512)S(1)}, f32[512]{0:T(512)S(1)}, /*index=5*/f32[512]{0:T(512)S(1)}) fusion(pred[512,1024]{1,0:T(32,128)(4,1)} %copy.172, f32[512,1024]{1,0:T(8,128)} %get-tuple-element.198, f32[512]{0:T(512)S(1)} %get-tuple-element.136, f32[512]{0:T(512)S(1)} %get-tuple-element.134, ...), kind=kLoop, calls=%fused_computation.200 | loop fusion | flops 15725568 | bytes 13131776 | tf_op jit(solution)/shard_map/reduce_sum | solution.py:141
  405.0 9.3 %fusion.119 = (f32[512]{0:T(512)S(1)}, f32[512]{0:T(512)S(1)}, f32[512]{0:T(512)S(1)}, f32[512]{0:T(512)S(1)}, f32[512]{0:T(512)S(1)}, /*index=5*/f32[512]{0:T(512)S(1)}) fusion(pred[512,1024]{1,0:T(32,128)(4,1)} %copy.174, f32[512,1024]{1,0:T(8,128)} %get-tuple-element.197, f32[512]{0:T(512)S(1)} %get-tuple-element.135, f32[512]{0:T(512)S(1)} %get-tuple-element.133, ...), kind=kLoop, calls=%fused_computation.202 | loop fusion | flops 15725568 | bytes 13131776 | tf_op jit(solution)/shard_map/reduce_sum | solution.py:141
  459.0 9.4 %convolution_convert_fusion = bf16[1024,3072]{1,0:T(8,128)(2,1)} fusion(bf16[1024,768]{0,1:T(8,128)(2,1)S(1)} %bitcast.461, bf16[768,3072]{1,0:T(8,128)(2,1)} %all-gather.9.cloned.1.call-done), kind=kOutput, calls=%fused_computation.15 | convolution fusion | flops 4834983936 | bytes 12582912 | tf_op jit(solution)/shard_map/dot_general | solution.py:154
  468.4 146.0 %reduce-scatter.2.cloned.1.call-done = bf16[256,3072]{1,0:T(8,128)(2,1)} async-done(((bf16[1024,3072]{1,0:T(8,128)(2,1)}), bf16[256,3072]{1,0:T(8,128)(2,1)}) %reduce-scatter.2.cloned.1.call-update) | async-done | bytes 1572880 | tf_op jit(solution)/shard_map/reduce_scatter | solution.py:153
  (254 shorter events, 113.7 us)
Async XLA Ops:
  6.5 7.6 %copy-start = (bf16[256,3,192]{0,2,1:T(8,128)(2,1)S(1)}, bf16[256,3,192]{0,2,1:T(8,128)(2,1)}, u32[]{:S(2)}) copy-start(bf16[256,3,192]{0,2,1:T(8,128)(2,1)} %param.12) | copy-start | bytes 884740
  6.5 121.4 %all-gather.5.cloned.1.call-start = ((), (), s32[]{:S(2)}) async-start(), calls=%async_computation.1 | async-start | bytes 7864320 | tf_op jit(solution)/shard_map/all_gather | solution.py:103
  7.3 211.7 %all-gather.7.cloned.1.call-start = ((), (), s32[]{:S(2)}) async-start(), calls=%async_computation.2 | async-start | bytes 17694720 | tf_op jit(solution)/shard_map/all_gather | solution.py:96
  13.4 445.6 %all-gather.9.cloned.1.call-start = ((), (), s32[]{:S(2)}) async-start(), calls=%async_computation.3 | async-start | bytes 5898240 | tf_op jit(solution)/shard_map/all_gather | solution.py:97
  127.9 4.6 copy-start.2
  242.3 20.3 %copy-start.39 = (s32[4,16]{1,0:T(4,128)S(1)}, s32[4,16]{1,0:T(4,128)}, u32[]{:S(2)}) copy-start(s32[4,16]{1,0:T(4,128)} %param.15) | copy-start | bytes 772
  244.4 31.0 %collective-permute-start = (bf16[1,1024,1536]{1,2,0:T(8,128)(2,1)S(1)}, bf16[1,1024,1536]{1,2,0:T(8,128)(2,1)}, u32[]{:S(2)}, u32[]{:S(2)}) collective-permute-start(bf16[1,1024,1536]{1,2,0:T(8,128)(2,1)S(1)} %slice_bitcast_fusion), channel_id=1, source_target_pairs={{0,4},{4,8},{8,12},{1,5},{5,9},{9,13},{2,6},{6,10},{10,14},{3,7},{... | collective-permute-start | bytes 9437192 | tf_op jit(solution)/shard_map/ppermute | solution.py:18
  248.3 27.1 %collective-permute-start.1 = (bf16[1,1024,1536]{1,2,0:T(8,128)(2,1)S(1)}, bf16[1,1024,1536]{1,2,0:T(8,128)(2,1)}, u32[]{:S(2)}, u32[]{:S(2)}) collective-permute-start(bf16[1,1024,1536]{1,2,0:T(8,128)(2,1)S(1)} %slice_bitcast_fusion), channel_id=1, source_target_pairs={{4,0},{8,4},{12,8},{5,1},{9,5},{13,9},{6,2},{10,6},{14,10},{7,3},{... | collective-permute-start | bytes 9437192 | tf_op jit(solution)/shard_map/ppermute | solution.py:21
  249.6 364.8 %reduce-scatter.2.cloned.1.call-start = ((), (), s32[]{:S(2)}) async-start(), calls=%async_computation.4 | async-start | bytes 7864320 | tf_op jit(solution)/shard_map/reduce_scatter | solution.py:153
  303.3 32.8 %copy-start.7 = (f32[512,1024]{1,0:T(8,128)}, f32[512,1024]{1,0:T(8,128)S(1)}, u32[]{:S(2)}) copy-start(f32[512,1024]{1,0:T(8,128)S(1)} %fusion.221) | copy-start | bytes 6291460
  325.7 5.0 copy-start.28
  330.7 5.4 copy-start.29
  370.6 5.3 copy-start.4
  370.6 5.3 copy-start.34
  375.9 4.7 copy-start.32
  385.4 10.2 %copy-start.5 = (f32[512,1024]{1,0:T(8,128)S(1)}, f32[512,1024]{1,0:T(8,128)}, u32[]{:S(2)}) copy-start(f32[512,1024]{1,0:T(8,128)} %fusion.218) | copy-start | bytes 6291460
  385.4 10.2 %copy-start.13 = (f32[512,1024]{1,0:T(8,128)S(1)}, f32[512,1024]{1,0:T(8,128)}, u32[]{:S(2)}) copy-start(f32[512,1024]{1,0:T(8,128)} %fusion.224) | copy-start | bytes 6291460
  395.7 9.3 %copy-start.12 = (f32[512,1024]{1,0:T(8,128)S(1)}, f32[512,1024]{1,0:T(8,128)}, u32[]{:S(2)}) copy-start(f32[512,1024]{1,0:T(8,128)} %fusion.226) | copy-start | bytes 6291460
  414.3 2.9 copy-start.18
  424.8 5.4 slice-start
  426.7 3.5 slice-start.1
  468.4 146.0 %copy-start.27 = (bf16[256,3072]{1,0:T(8,128)(2,1)S(1)}, bf16[256,3072]{1,0:T(8,128)(2,1)}, u32[]{:S(2)}) copy-start(bf16[256,3072]{1,0:T(8,128)(2,1)} %param.9) | copy-start | bytes 4718596
  468.4 146.0 %copy-start.38 = (f32[1,3072]{1,0:T(1,128)S(1)}, f32[1,3072]{1,0:T(1,128)}, u32[]{:S(2)}) copy-start(f32[1,3072]{1,0:T(1,128)} %get-tuple-element.149) | copy-start | bytes 36868
  614.4 3.2 copy-start.1
  (26 other events, 44.8 us)
Sparse Core Ops, SparseCore 0:
  8.9 118.9 all-gather.4
  129.5 89.4 all-gather.6
  249.7 50.9 all-gather.8
  468.5 145.8 reduce-scatter.1
where the time goes:
time: 633 us; the launch traced here: 624 us
  waiting for transfers between devices  307 us (48%)
  matrix products  136 us (21%)
  other arithmetic  72.7 us (11%)
  local copies, waits for them, and re-layouts  39.1 us (6%)
  blocking collectives  37.1 us (6%)
  starting transfers between devices  17.5 us (3%)
  between operations  15.1 us (2%)
    reduce_scatter x1, waiting for transfers between devices, body(): lax.psum_scatter(jnp.dot(attended, out_full, preferred_element_type=jnp.f...  146 us
    all_gather x1, waiting for transfers between devices, body(): qkv_full = lax.all_gather(qkv_weight, 'seq', axis=0, tiled=True)  84.6 us
    all_gather x1, waiting for transfers between devices, body(): lax.all_gather(latents, 'fsdp', axis=0, tiled=True)  75.7 us
    dot_general x36, matrix products, body(): lax.dot_general(queries, key_all[key_blk, :, head_idx], (((1,), (1,)), ((...  65 us
    reduce_sum x6, other arithmetic, body(): running_total = running_total * factor + jnp.sum(weights, axis=1)  52 us
    dot_general x36, matrix products, body(): jnp.dot(weights.astype(jnp.bfloat16), value_all[key_blk, :, head_idx], pr...  41 us
    all_gather x1, blocking collectives, body(): modulation = lax.all_gather(own_mod, ('seq', 'fsdp'), axis=1, tiled=True)  37.1 us
    dot_general x1, matrix products, project_rows(): mixture = jnp.dot(normed, weight_flat, preferred_element_type=jnp.float32)  20 us
  transfers between devices with their start and end apart: 6, of which 3 were waited for; matrix products, arithmetic and copies ran while one was open for 32% of the time, Pallas kernels for 0%

commit v1 on v0

--- a/solution.py
+++ b/solution.py
@@ -93,7 +93,12 @@
     shift_mod = modulation[0]
     scale_mod = modulation[1]
     gate_mod = modulation[2]
-    qkv_full = lax.all_gather(qkv_weight, "seq", axis=0, tiled=True)
+    ring = [qkv_weight]
+    for hop in range(3):
+        ring.append(lax.ppermute(ring[-1], "seq", [(dev, (dev + 1) % 4) for dev in range(4)]))
+    qkv_full = jnp.roll(
+        jnp.concatenate(ring[::-1], axis=0), (lax.axis_index("seq") + 1) * ring[0].shape[0], axis=0
+    )
     out_full = lax.all_gather(out_weight, "seq", axis=1, tiled=True)
     model_width = qkv_full.shape[0]
     group_width = qkv_full.shape[2]

time: 633 us -> 605 us (0.956)
  waiting for transfers between devices: 307 us -> 241 us
  local copies, waits for them, and re-layouts: 39.1 us -> 79.4 us
  starting transfers between devices: 17.5 us -> 5.71 us
  other arithmetic: 72.7 us -> 79.5 us
    all_gather x1 -> x0, waiting for transfers between devices: 84.6 us -> none  [body(): qkv_full = lax.all_gather(qkv_weight, 'seq', axis=0, tiled=True)]
    ppermute x0 -> x3, waiting for transfers between devices: none -> 82.3 us  [body(): lax.ppermute(ring[-1], 'seq', [(dev, (dev + 1) % 4) for dev in range(4)])]
    all_gather x1, waiting for transfers between devices: 75.7 us -> 0.01 us  [body(): lax.all_gather(latents, 'fsdp', axis=0, tiled=True)]
    unnamed x91 -> x124, local copies, waits for them, and re-layouts: 17.7 us -> 40.2 us
    dynamic_slice x0 -> x1, local copies, waits for them, and re-layouts: none -> 15.8 us  [body(): jnp.roll(jnp.concatenate(ring[::-1], axis=0), (lax.axis_index('seq') + 1)...]
    reduce_scatter x1, starting transfers between devices: 12.3 us -> 0.21 us  [body(): lax.psum_scatter(jnp.dot(attended, out_full, preferred_element_type=jnp.f...]
    reduce_scatter x1, waiting for transfers between devices: 146 us -> 158 us  [body(): lax.psum_scatter(jnp.dot(attended, out_full, preferred_element_type=jnp.f...]
    dot_general x36, matrix products: 41 us -> 47.5 us  [body(): jnp.dot(weights.astype(jnp.bfloat16), value_all[key_blk, :, head_idx], pr...]
  transfers between devices with their start and end apart: 6 -> 8, of which waited for: 3 -> 3; matrix products, arithmetic and copies ran while one was open for 32% -> 36% of each run, Pallas kernels for 0% -> 0%
where the time goes in v1:
time: 605 us; the launch traced here: 599 us
  waiting for transfers between devices  241 us (40%)
  matrix products  141 us (23%)
  other arithmetic  79.5 us (13%)
  local copies, waits for them, and re-layouts  79.4 us (13%)
  blocking collectives  36.2 us (6%)
  between operations  17 us (3%)
    reduce_scatter x1, waiting for transfers between devices, body(): lax.psum_scatter(jnp.dot(attended, out_full, preferred_element_type=jnp.f...  158 us
    ppermute x3, waiting for transfers between devices, body(): lax.ppermute(ring[-1], 'seq', [(dev, (dev + 1) % 4) for dev in range(4)])  82.3 us
    dot_general x36, matrix products, body(): lax.dot_general(queries, key_all[key_blk, :, head_idx], (((1,), (1,)), ((...  64.9 us
    reduce_sum x6, other arithmetic, body(): running_total = running_total * factor + jnp.sum(weights, axis=1)  53.4 us
    dot_general x36, matrix products, body(): jnp.dot(weights.astype(jnp.bfloat16), value_all[key_blk, :, head_idx], pr...  47.5 us
    unnamed x124, local copies, waits for them, and re-layouts  40.2 us
    all_gather x1, blocking collectives, body(): modulation = lax.all_gather(own_mod, ('seq', 'fsdp'), axis=1, tiled=True)  36.2 us
    dot_general x1, matrix products, project_rows(): mixture = jnp.dot(normed, weight_flat, preferred_element_type=jnp.float32)  18.8 us
  transfers between devices with their start and end apart: 8, of which 3 were waited for; matrix products, arithmetic and copies ran while one was open for 36% of the time, Pallas kernels for 0%

profile of v1, /device:TPU:0, one launch (start us, length us, event | category | flops | bytes accessed | tf_op | source)
XLA Modules:
  0.0 599.3 jit_solution(7494153632940384450)
XLA Ops:
  8.1 6.0 %copy.167 = bf16[768,3,768]{0,2,1:T(8,128)(2,1)} copy(bf16[768,3,768]{2,0,1:T(8,128)(2,1)} %param.10) | data formatting | bytes 7077888 | tf_op args[1]
  14.6 41.3 %collective-permute-done = bf16[768,3,768]{0,2,1:T(8,128)(2,1)S(1)} collective-permute-done((bf16[768,3,768]{0,2,1:T(8,128)(2,1)}, bf16[768,3,768]{0,2,1:T(8,128)(2,1)S(1)}, u32[]{:S(2)}, u32[]{:S(2)}) %collective-permute-start) | collective-permute-done | bytes 3538976 | tf_op jit(solution)/shard_map/ppermute | solution.py:98
  57.8 41.0 %collective-permute-done.1 = bf16[768,3,768]{0,2,1:T(8,128)(2,1)} collective-permute-done((bf16[768,3,768]{0,2,1:T(8,128)(2,1)S(1)}, bf16[768,3,768]{0,2,1:T(8,128)(2,1)}, u32[]{:S(2)}, u32[]{:S(2)}) %collective-permute-start.1) | collective-permute-done | bytes 3538976 | tf_op jit(solution)/shard_map/ppermute | solution.py:98
  99.7 36.2 %all-gather = f32[16,192,3]{1,2,0:T(4,128)S(1)} all-gather(f32[1,192,3]{1,2,0:T(4,128)S(1)} %bitcast.465), channel_id=1, replica_groups=mesh['group'=2,'seq'=4,'fsdp'=4] {'seq','fsdp'}, dimensions={0}, use_global_device_ids=true | all-gather | bytes 39168 | tf_op jit(solution)/shard_map/all_gather | solution.py:92
  147.1 4.2 constant_dynamic-update-slice_fusion.6
  160.8 4.2 constant_dynamic-update-slice_fusion.2
  169.2 15.8 %constant_dynamic-slice_fusion.1 = bf16[3072,3,768]{0,2,1:T(8,128)(2,1)} fusion(bf16[6144,3,768]{0,2,1:T(8,128)(2,1)} %constant_dynamic-update-slice_fusion, s32[]{:T(128)S(6)} %select_n.279), kind=kLoop, calls=%fused_computation.467 | loop fusion | bytes 28311556 | tf_op jit(solution)/shard_map/jit(_roll_dynamic)/dynamic_slice | solution.py:99
  185.0 18.8 %fusion.7 = f32[1024,3,6,128]{0,3,2,1:T(8,128)S(1)} fusion(bf16[3,6,128,3072]{3,2,1,0:T(8,128)(2,1)} %bitcast.417, bf16[1024,3072]{1,0:T(8,128)(2,1)S(1)} %copy-done.3, f32[3072]{0:T(1024)S(1)} %bitcast.466, f32[3072]{0:T(1024)S(1)} %bitcast.467, f32[1024]{0:T(1024)S(1)} %add_rsqrt_fusion.2, f32[1024]{0:T(1024)S(1)} %broadcast_multiply_fusion), kind=kOutput, calls=%fused_computation.10 | convolution fusion | flops 14514388992 | bytes 29917184 | tf_op jit(solution)/shard_map/dot_general | solution.py:46
  227.9 8.0 %pad_maximum_fusion = bf16[3,1024,1536]{1,2,0:T(8,128)(2,1)} fusion(bf16[1,1024,1536]{1,2,0:T(8,128)(2,1)} %collective-permute-done.4, bf16[1,1024,1536]{1,2,0:T(8,128)(2,1)S(1)} %slice_bitcast_fusion, bf16[1,1024,1536]{1,2,0:T(8,128)(2,1)} %collective-permute-done.3), kind=kLoop, calls=%fused_computation.8 | loop fusion | flops 9437184 | bytes 18874368 | tf_op jit(solution)/shard_map/concatenate | solution.py:22
  235.8 7.1 %fusion.406 = (bf16[3,1024,768]{1,2,0:T(8,128)(2,1)}, bf16[3,1024,768]{1,2,0:T(8,128)(2,1)S(1)}) fusion(bf16[3,1024,1536]{1,2,0:T(8,128)(2,1)} %pad_maximum_fusion), kind=kLoop, calls=%fused_computation.643 | loop fusion | bytes 18874368 | tf_op jit(solution)/shard_map/slice | solution.py:118
  278.2 5.0 fusion.43
  283.2 5.4 fusion.44
  288.6 4.7 fusion.45
  295.6 10.1 %fusion.109 = (f32[512]{0:T(512)S(1)}, f32[512]{0:T(512)S(1)}, f32[512]{0:T(512)S(1)}, f32[512]{0:T(512)S(1)}, f32[512]{0:T(512)S(1)}, /*index=5*/f32[512]{0:T(512)S(1)}) fusion(pred[512,1024]{1,0:T(32,128)(4,1)} %copy.170, f32[512,1024]{1,0:T(8,128)} %get-tuple-element.202, f32[512]{0:T(512)S(1)} %get-tuple-element.167, f32[512]{0:T(512)S(1)} %get-tuple-element.166, ...), kind=kLoop, calls=%fused_computation.192 | loop fusion | flops 15725568 | bytes 13131776 | tf_op jit(solution)/shard_map/reduce_sum | solution.py:146
  305.7 6.6 %fusion.111 = (f32[512]{0:T(512)S(1)}, f32[512]{0:T(512)S(1)}, f32[512]{0:T(512)S(1)}, f32[512]{0:T(512)S(1)}, f32[512]{0:T(512)S(1)}, /*index=5*/f32[512]{0:T(512)S(1)}) fusion(pred[512,1024]{1,0:T(32,128)(4,1)S(1)} %copy-done.32, f32[512,1024]{1,0:T(8,128)} %get-tuple-element.201, f32[512]{0:T(512)S(1)} %get-tuple-element.121, ...), kind=kLoop, calls=%fused_computation.194 | loop fusion | flops 15725568 | bytes 13131776 | tf_op jit(solution)/shard_map/reduce_sum | solution.py:146
  312.3 6.6 %fusion.113 = (f32[512]{0:T(512)S(1)}, f32[512]{0:T(512)S(1)}, f32[512]{0:T(512)S(1)}, f32[512]{0:T(512)S(1)}, f32[512]{0:T(512)S(1)}, /*index=5*/f32[512]{0:T(512)S(1)}) fusion(pred[512,1024]{1,0:T(32,128)(4,1)S(1)} %copy-done.33, f32[512,1024]{1,0:T(8,128)} %get-tuple-element.200, f32[512]{0:T(512)S(1)} %get-tuple-element.120, ...), kind=kLoop, calls=%fused_computation.196 | loop fusion | flops 15725568 | bytes 13131776 | tf_op jit(solution)/shard_map/reduce_sum | solution.py:146
  325.5 5.3 fusion.46
  330.8 4.7 fusion.47
  335.6 4.7 fusion.48
  343.2 10.2 %fusion.115 = (f32[512]{0:T(512)S(1)}, f32[512]{0:T(512)S(1)}, f32[512]{0:T(512)S(1)}, f32[512]{0:T(512)S(1)}, f32[512]{0:T(512)S(1)}, /*index=5*/f32[512]{0:T(512)S(1)}) fusion(pred[512,1024]{1,0:T(32,128)(4,1)} %copy.176, f32[512,1024]{1,0:T(8,128)} %get-tuple-element.199, f32[512]{0:T(512)S(1)} %get-tuple-element.180, f32[512]{0:T(512)S(1)} %get-tuple-element.179, ...), kind=kLoop, calls=%fused_computation.198 | loop fusion | flops 15725568 | bytes 13131776 | tf_op jit(solution)/shard_map/reduce_sum | solution.py:146
  353.5 9.8 %fusion.117 = (f32[512]{0:T(512)S(1)}, f32[512]{0:T(512)S(1)}, f32[512]{0:T(512)S(1)}, f32[512]{0:T(512)S(1)}, f32[512]{0:T(512)S(1)}, /*index=5*/f32[512]{0:T(512)S(1)}) fusion(pred[512,1024]{1,0:T(32,128)(4,1)} %copy.178, f32[512,1024]{1,0:T(8,128)} %get-tuple-element.198, f32[512]{0:T(512)S(1)} %get-tuple-element.136, f32[512]{0:T(512)S(1)} %get-tuple-element.134, ...), kind=kLoop, calls=%fused_computation.200 | loop fusion | flops 15725568 | bytes 13131776 | tf_op jit(solution)/shard_map/reduce_sum | solution.py:146
  363.3 10.1 %fusion.119 = (f32[512]{0:T(512)S(1)}, f32[512]{0:T(512)S(1)}, f32[512]{0:T(512)S(1)}, f32[512]{0:T(512)S(1)}, f32[512]{0:T(512)S(1)}, /*index=5*/f32[512]{0:T(512)S(1)}) fusion(pred[512,1024]{1,0:T(32,128)(4,1)} %copy.180, f32[512,1024]{1,0:T(8,128)} %get-tuple-element.197, f32[512]{0:T(512)S(1)} %get-tuple-element.135, f32[512]{0:T(512)S(1)} %get-tuple-element.133, ...), kind=kLoop, calls=%fused_computation.202 | loop fusion | flops 15725568 | bytes 13131776 | tf_op jit(solution)/shard_map/reduce_sum | solution.py:146
  421.4 9.4 %convolution_convert_fusion = bf16[1024,3072]{1,0:T(8,128)(2,1)} fusion(bf16[1024,768]{0,1:T(8,128)(2,1)S(1)} %bitcast.462, bf16[768,3072]{1,0:T(8,128)(2,1)} %all-gather.6.cloned.1.call-done), kind=kOutput, calls=%fused_computation.15 | convolution fusion | flops 4834983936 | bytes 12582912 | tf_op jit(solution)/shard_map/dot_general | solution.py:159
  430.8 157.7 %reduce-scatter.2.cloned.1.call-done = bf16[256,3072]{1,0:T(8,128)(2,1)} async-done(((bf16[1024,3072]{1,0:T(8,128)(2,1)}), bf16[256,3072]{1,0:T(8,128)(2,1)}) %reduce-scatter.2.cloned.1.call-update) | async-done | bytes 1572880 | tf_op jit(solution)/shard_map/reduce_scatter | solution.py:158
  (292 shorter events, 149.5 us)
Async XLA Ops:
  7.4 92.2 %copy-start = (bf16[256,3,192]{0,2,1:T(8,128)(2,1)S(1)}, bf16[256,3,192]{0,2,1:T(8,128)(2,1)}, u32[]{:S(2)}) copy-start(bf16[256,3,192]{0,2,1:T(8,128)(2,1)} %param.12) | copy-start | bytes 884740
  7.4 129.3 %all-gather.4.cloned.1.call-start = ((), (), s32[]{:S(2)}) async-start(), calls=%async_computation.1 | async-start | bytes 7864320 | tf_op jit(solution)/shard_map/all_gather | solution.py:108
  8.1 413.3 %all-gather.6.cloned.1.call-start = ((), (), s32[]{:S(2)}) async-start(), calls=%async_computation.2 | async-start | bytes 5898240 | tf_op jit(solution)/shard_map/all_gather | solution.py:102
  14.2 41.8 %collective-permute-start = (bf16[768,3,768]{0,2,1:T(8,128)(2,1)}, bf16[768,3,768]{0,2,1:T(8,128)(2,1)S(1)}, u32[]{:S(2)}, u32[]{:S(2)}) collective-permute-start(bf16[768,3,768]{0,2,1:T(8,128)(2,1)} %copy.167), channel_id=1, source_target_pairs={{0,4},{4,8},{8,12},{12,0},{1,5},{5,9},{9,13},{13,1},{2,6},{6,10},{... | collective-permute-start | bytes 10616840 | tf_op jit(solution)/shard_map/ppermute | solution.py:98
  57.8 41.0 %collective-permute-start.1 = (bf16[768,3,768]{0,2,1:T(8,128)(2,1)S(1)}, bf16[768,3,768]{0,2,1:T(8,128)(2,1)}, u32[]{:S(2)}, u32[]{:S(2)}) collective-permute-start(bf16[768,3,768]{0,2,1:T(8,128)(2,1)S(1)} %collective-permute-done), channel_id=1, source_target_pairs={{0,4},{4,8},{8,12},{12,0},{1,5},{5,9},{9,13},{13,1},{2,6},{6,10},{... | collective-permute-start | bytes 10616840 | tf_op jit(solution)/shard_map/ppermute | solution.py:98
  98.8 44.3 %collective-permute-start.2 = (bf16[768,3,768]{0,2,1:T(8,128)(2,1)}, bf16[768,3,768]{0,2,1:T(8,128)(2,1)}, u32[]{:S(2)}, u32[]{:S(2)}) collective-permute-start(bf16[768,3,768]{0,2,1:T(8,128)(2,1)} %collective-permute-done.1), channel_id=1, source_target_pairs={{0,4},{4,8},{8,12},{12,0},{1,5},{5,9},{9,13},{13,1},{2,6},{6,10},{... | collective-permute-start | bytes 10616840 | tf_op jit(solution)/shard_map/ppermute | solution.py:98
  136.7 4.6 copy-start.3
  147.1 4.2 copy-start.24
  207.0 8.0 %copy-start.52 = (s32[4,16]{1,0:T(4,128)S(1)}, s32[4,16]{1,0:T(4,128)}, u32[]{:S(2)}) copy-start(s32[4,16]{1,0:T(4,128)} %param.15) | copy-start | bytes 772
  209.2 18.7 %collective-permute-start.3 = (bf16[1,1024,1536]{1,2,0:T(8,128)(2,1)S(1)}, bf16[1,1024,1536]{1,2,0:T(8,128)(2,1)}, u32[]{:S(2)}, u32[]{:S(2)}) collective-permute-start(bf16[1,1024,1536]{1,2,0:T(8,128)(2,1)S(1)} %slice_bitcast_fusion), channel_id=1, source_target_pairs={{0,4},{4,8},{8,12},{1,5},{5,9},{9,13},{2,6},{6,10},{10,14},{3,7},{... | collective-permute-start | bytes 9437192 | tf_op jit(solution)/shard_map/ppermute | solution.py:18
  212.8 15.0 %collective-permute-start.4 = (bf16[1,1024,1536]{1,2,0:T(8,128)(2,1)S(1)}, bf16[1,1024,1536]{1,2,0:T(8,128)(2,1)}, u32[]{:S(2)}, u32[]{:S(2)}) collective-permute-start(bf16[1,1024,1536]{1,2,0:T(8,128)(2,1)S(1)} %slice_bitcast_fusion), channel_id=1, source_target_pairs={{4,0},{8,4},{12,8},{5,1},{9,5},{13,9},{6,2},{10,6},{14,10},{7,3},{... | collective-permute-start | bytes 9437192 | tf_op jit(solution)/shard_map/ppermute | solution.py:21
  214.1 374.4 %reduce-scatter.2.cloned.1.call-start = ((), (), s32[]{:S(2)}) async-start(), calls=%async_computation.3 | async-start | bytes 7864320 | tf_op jit(solution)/shard_map/reduce_scatter | solution.py:158
  255.9 32.7 %copy-start.8 = (f32[512,1024]{1,0:T(8,128)}, f32[512,1024]{1,0:T(8,128)S(1)}, u32[]{:S(2)}) copy-start(f32[512,1024]{1,0:T(8,128)S(1)} %fusion.221) | copy-start | bytes 6291460
  278.2 5.0 copy-start.32
  283.2 5.4 copy-start.33
  325.5 5.3 copy-start.5
  325.5 5.3 copy-start.38
  330.8 4.8 copy-start.36
  343.2 10.2 %copy-start.6 = (f32[512,1024]{1,0:T(8,128)S(1)}, f32[512,1024]{1,0:T(8,128)}, u32[]{:S(2)}) copy-start(f32[512,1024]{1,0:T(8,128)} %fusion.218) | copy-start | bytes 6291460
  343.2 10.2 %copy-start.15 = (f32[512,1024]{1,0:T(8,128)S(1)}, f32[512,1024]{1,0:T(8,128)}, u32[]{:S(2)}) copy-start(f32[512,1024]{1,0:T(8,128)} %fusion.224) | copy-start | bytes 6291460
  353.4 9.8 %copy-start.13 = (f32[512,1024]{1,0:T(8,128)S(1)}, f32[512,1024]{1,0:T(8,128)}, u32[]{:S(2)}) copy-start(f32[512,1024]{1,0:T(8,128)} %fusion.226) | copy-start | bytes 6291460
  395.0 5.4 slice-start
  430.8 157.7 %copy-start.31 = (bf16[256,3072]{1,0:T(8,128)(2,1)S(1)}, bf16[256,3072]{1,0:T(8,128)(2,1)}, u32[]{:S(2)}) copy-start(bf16[256,3072]{1,0:T(8,128)(2,1)} %param.9) | copy-start | bytes 4718596
  430.8 157.7 %copy-start.42 = (f32[1,3072]{1,0:T(1,128)S(1)}, f32[1,3072]{1,0:T(1,128)}, u32[]{:S(2)}) copy-start(f32[1,3072]{1,0:T(1,128)} %get-tuple-element.149) | copy-start | bytes 36868
  (41 other events, 77.3 us)
Sparse Core Ops, SparseCore 0:
  9.8 119.0 all-gather.3
  431.0 157.4 reduce-scatter.1
Sparse Core Ops, SparseCore 1:
  214.2 49.9 all-gather.5
